TPU v7x, 128 devices: a whole 4x4x4 slice. The times are simulated.
128 devices in a mesh: gx: 32 (over x_hi, z, y), gy: 4 (over x_lo, core).
Axes of the slice: x: 4 (x_hi: 2, x_lo: 2; x = x_hi * 2 + x_lo), y: 4, z: 4, core: 2. Of those that a mesh axis runs over, the one named last changes fastest.
Arguments:
- populations: float32 [27, 256, 128, 128], P(None, 'gx', 'gy'), may hold values from 0.49 to 1.69
- precursor: float32 [27, 64, 128, 128], P(None, 'gx', 'gy'), may hold values from 0.49 to 1.69
- pairing: int32 [32], replicated, may hold values from 0 to 31, each once
- rates: float32 [27], replicated, may hold values from 0.5 to 1.9
- loading: float32 [32], replicated, may hold values from 4 to 32
- disc_cols: int32 [512], replicated, may hold values from 0 to 32767, as said below
- disc_turb: int32 [512], replicated, may hold values from -1 to 31, as said below
Outputs:
- read: float32 [27, 256, 128, 128], P(None, 'gx', 'gy')
- disc_speed: float32 [32], replicated
Inputs may be any that keep to these rules, and one draw needn't show every extreme that they name: `disc_cols`: each turbine's used slots name 8 to 16 spanwise-adjacent columns (periodic in y) of one streamwise plane; unused slots hold column 0. `disc_turb`: every turbine id 0..31 has 8 to 16 used slots, both counts reached; -1 marks an unused slot; slots are in no particular order.
All inputs are finite; a program needn't handle non-finite values.
Results may differ from a plain program's by a relative error of at most 0.00009.
Values sent between devices are 32-bit elements; how exact they have to be, the bound alone decides.
No kernel may reach another device: no remote copies, remote signals or barrier semaphores. Data moves between devices by JAX's collectives and lax.ppermute only.
A program may use at most 128 MiB of HBM per device.

v0:
```python
import jax
import jax.numpy as jnp
import numpy as np
from jax import lax
from jax.sharding import PartitionSpec as P

FULL_PRECISION = lax.Precision.HIGHEST


def extended(cells, sides, width):
    for axis, dim in sides:
        count = lax.axis_size(axis)
        head = lax.slice_in_dim(cells, 0, width, axis=dim)
        tail = lax.slice_in_dim(cells, cells.shape[dim] - width, cells.shape[dim], axis=dim)
        cells = jnp.concatenate(
            [
                lax.ppermute(tail, axis, [(i, (i + 1) % count) for i in range(count)]),
                cells,
                lax.ppermute(head, axis, [((i + 1) % count, i) for i in range(count)]),
            ],
            axis=dim,
        )
    return cells


def lattice_tables():
    steps_one = np.array([-1.0, 0.0, 1.0])
    weight_one = np.array([1.0 / 6.0, 2.0 / 3.0, 1.0 / 6.0])
    grid_x, grid_y, grid_z = np.meshgrid(np.arange(3), np.arange(3), np.arange(3), indexing="ij")
    grid_x = grid_x.ravel()
    grid_y = grid_y.ravel()
    grid_z = grid_z.ravel()
    shift_x = steps_one[grid_x]
    shift_y = steps_one[grid_y]
    shift_z = steps_one[grid_z]
    weights = weight_one[grid_x] * weight_one[grid_y] * weight_one[grid_z]
    vander = np.array([[1.0, 1.0, 1.0], [-1.0, 0.0, 1.0], [1.0, 0.0, 1.0]])
    inverse = np.array([[0.0, -0.5, 0.5], [1.0, 0.0, -1.0], [0.0, 0.5, 0.5]])
    moment_map = np.kron(np.kron(vander, vander), vander) * weights[None, :]
    back_map = np.kron(np.kron(inverse, inverse), inverse) / weights[:, None]
    third = 1.0 / 3.0
    fringe_map = np.stack(
        [
            weights,
            weights * shift_x,
            weights * shift_y,
            weights * shift_z,
            weights * shift_x * shift_x,
            weights * shift_y * shift_y,
            weights * shift_z * shift_z,
            weights * shift_x * shift_y,
            weights * shift_x * shift_z,
            weights * shift_y * shift_z,
        ]
    )
    quad_x = shift_x * shift_x - third
    quad_y = shift_y * shift_y - third
    quad_z = shift_z * shift_z - third
    rebuild_map = np.stack(
        [
            1.0 - 1.5 * (quad_x + quad_y + quad_z),
            3.0 * shift_x,
            3.0 * shift_y,
            3.0 * shift_z,
            4.5 * quad_x,
            4.5 * quad_y,
            4.5 * quad_z,
            9.0 * shift_x * shift_y,
            9.0 * shift_x * shift_z,
            9.0 * shift_y * shift_z,
        ],
        axis=1,
    )
    tables = (shift_x, shift_y, shift_z, moment_map, back_map, fringe_map, rebuild_map)
    return tuple((jnp.asarray(table, dtype=jnp.float32) for table in tables))


def disc_profile(depth):
    heights = jnp.arange(depth).astype(jnp.float32)
    return jnp.exp(-jnp.square((heights - depth / 3.0) / (depth / 6.0)))


def relax_cells(tables, moments, rates, force):
    shift_x, shift_y, shift_z, moment_map, back_map = tables[:5]
    density = moments[0]
    velocity_x = moments[9] / density
    velocity_y = moments[3] / density
    velocity_z = moments[1] / density
    projected = (
        shift_x[:, None] * velocity_x[None, :]
        + shift_y[:, None] * velocity_y[None, :]
        + shift_z[:, None] * velocity_z[None, :]
    )
    speed_sq = velocity_x * velocity_x + velocity_y * velocity_y + velocity_z * velocity_z
    balance = density[None, :] * (
        1.0 + 3.0 * projected + 4.5 * projected * projected - 1.5 * speed_sq[None, :]
    )
    balance_moments = jnp.dot(moment_map, balance, precision=FULL_PRECISION)
    relaxed = moments - rates[:, None] * (moments - balance_moments)
    return (
        jnp.dot(back_map, relaxed, precision=FULL_PRECISION)
        + 3.0 * shift_x[:, None] * force[None, :]
    )


def body(populations, precursor, pairing, rates, loading, disc_cols, disc_turb):
    tables = lattice_tables()
    comps, width_x, width_y, depth = populations.shape
    fringe_width = precursor.shape[1]
    turbines = loading.shape[0]
    flat = populations.reshape(comps, width_x * width_y * depth)
    moments = jnp.dot(tables[3], flat, precision=FULL_PRECISION)
    velocity_x = moments[9] / moments[0]
    profile = disc_profile(depth)
    along_y = width_y * lax.axis_size("gy")
    tile_x = lax.axis_index("gx")
    tile_y = lax.axis_index("gy")
    local_x = disc_cols // along_y - tile_x * width_x
    local_y = disc_cols % along_y - tile_y * width_y
    owned = (
        (disc_turb >= 0)
        & (local_x >= 0)
        & (local_x < width_x)
        & (local_y >= 0)
        & (local_y < width_y)
    )
    local_cell = jnp.where(owned, local_x * width_y + local_y, 0)
    columns = velocity_x.reshape(width_x * width_y, depth)[local_cell]
    row_values = jnp.where(owned, jnp.dot(columns, profile, precision=FULL_PRECISION), 0.0)
    owner_table = (disc_turb[None, :] == jnp.arange(turbines, dtype=jnp.int32)[:, None]).astype(
        jnp.float32
    )
    partial_totals = jnp.dot(owner_table, row_values, precision=FULL_PRECISION)
    totals = lax.psum(partial_totals, ("gx", "gy"))
    counts = jnp.sum(owner_table, axis=1)
    disc_speed = totals / (counts * jnp.sum(profile))
    thrust = 0.5 * loading * disc_speed * jnp.abs(disc_speed)
    row_thrust = jnp.dot(thrust, owner_table, precision=FULL_PRECISION)
    placed = (
        (jnp.arange(width_x * width_y, dtype=jnp.int32)[:, None] == local_cell[None, :])
        & owned[None, :]
    ).astype(jnp.float32)
    column_force = jnp.dot(placed, row_thrust, precision=FULL_PRECISION)
    force = -(column_force[:, None] * profile[None, :]).reshape(width_x * width_y * depth)
    post = relax_cells(tables, moments, rates, force).reshape(comps, width_x, width_y, depth)
    source_tile = pairing[tile_x]
    wanted = source_tile * fringe_width + jnp.arange(fringe_width, dtype=jnp.int32)
    piece = lax.all_gather(precursor, "gx", axis=1, tiled=True)
    have = jnp.arange(piece.shape[1], dtype=jnp.int32)
    chosen = (wanted[:, None] == have[None, :]).astype(jnp.float32)
    chosen_pops = jnp.einsum("pr,kryz->kpyz", chosen, piece, precision=FULL_PRECISION)
    selected = jnp.dot(
        tables[5],
        chosen_pops.reshape(comps, fringe_width * width_y * depth),
        precision=FULL_PRECISION,
    )
    rebuilt = jnp.dot(
        tables[6], selected.reshape(10, fringe_width * width_y * depth), precision=FULL_PRECISION
    )
    rebuilt = rebuilt.reshape(comps, fringe_width, width_y, depth)
    blend = (0.5 / (jnp.arange(fringe_width).astype(jnp.float32) + 1.0))[None, :, None, None]
    head = (1.0 - blend) * post[:, :fringe_width] + blend * rebuilt
    post = jnp.concatenate([head, post[:, fringe_width:]], axis=1)
    pieces = []
    padded = extended(post, (("gx", 1), ("gy", 2)), 1)
    for slot in range(27):
        step_x = slot // 9 - 1
        step_y = slot // 3 % 3 - 1
        pieces.append(
            padded[slot, 1 - step_x : 1 - step_x + width_x, 1 - step_y : 1 - step_y + width_y]
        )
    finished = []
    for slot in range(27):
        step_z = slot % 3 - 1
        moved = pieces[slot]
        if step_z == 1:
            moved = jnp.concatenate([post[26 - slot][:, :, :1], moved[:, :, :-1]], axis=2)
        elif step_z == -1:
            moved = jnp.concatenate([moved[:, :, 1:], post[26 - slot][:, :, -1:]], axis=2)
        finished.append(moved)
    return (jnp.stack(finished), disc_speed)


def solution(mesh):
    in_specs = (P(None, "gx", "gy", None), P(None, "gx", "gy", None), P(), P(), P(), P(), P())
    out_specs = (P(None, "gx", "gy", None), P())
    return jax.shard_map(body, mesh=mesh, in_specs=in_specs, out_specs=out_specs, check_vma=False)
```

profile of v0, /device:TPU:121, one launch (start us, length us, event | category | flops | bytes accessed | tf_op | source)
XLA Modules:
  0.0 319.7 jit_solution(4355309923791451909)
XLA Ops:
  7.2 2.2 copy.22
  9.4 2.4 pad.213
  11.9 4.4 %copy.26 = f32[4,8,256,128]{3,1,2,0:T(8,128)} copy(f32[4,8,256,128]{3,2,1,0:T(8,128)S(1)} %bitcast.220) | data formatting | bytes 8388608
  16.4 5.4 %fusion.80 = f32[27,32768]{1,0:T(8,128)S(1)} fusion(f32[27,27]{1,0:T(8,128)S(1)} %copy-done.5, f32[27,32768]{1,0:T(8,128)} %bitcast.218), kind=kOutput, calls=%fused_computation.182 | convolution fusion | flops 286654464 | bytes 7080804 | tf_op jit(solution)/shard_map/dot_general | solution.py:112
  21.8 2.0 copy-done.2
  23.7 0.5 add_multiply_fusion
  24.3 1.0 gather_fusion
  25.3 0.3 fusion.66
  25.7 0.2 convolution_bitcast_fusion.1
  25.8 70.7 %psum.7 = f32[32]{0:T(128)S(1)} all-reduce(f32[32]{0:T(128)S(1)} %convolution_bitcast_fusion.1), channel_id=1, replica_groups=mesh['gx'=32,'gy'=4] {'gx','gy'}, use_global_device_ids=true, to_apply=%region_0.1 | all-reduce | flops 32 | bytes 256 | tf_op jit(solution)/shard_map/psum | solution.py:134
  96.6 0.6 fusion.73
  97.2 0.1 convert_reduce_fusion
  97.3 0.7 multiply_divide_fusion
  98.0 0.1 convolution_bitcast_fusion
  98.1 0.3 fusion.31
  98.5 7.5 %fusion.1 = f32[27,32768]{1,0:T(8,128)S(1)} fusion(f32[27,32768]{1,0:T(8,128)} %copy-done.2, f32[27,27]{1,0:T(8,128)S(1)} %copy-done.5, f32[32768]{0:T(1024)S(1)} %bitcast.250, f32[32768]{0:T(1024)S(1)} %bitcast.252, f32[27]{0:T(128)S(1)} %copy-done.15, f32[32768]{0:T(1024)S(1)} %bitcast.251, f32[27]{0:T(128)S(1)} %copy-done.16, f32[32768]{0:T(1024)S(1)} %bitcast.217, ...), kind=kOutput, calls=%fused_computation.4 | convolution fusion | flops 299925504 | bytes 7736596 | tf_op jit(solution)/shard_map/dot_general | solution.py:98
  106.1 0.1 negate_bitcast_fusion
  106.2 4.1 %convolution_add_fusion = f32[27,32768]{1,0:T(8,128)S(1)} fusion(f32[27,27]{1,0:T(8,128)S(1)} %copy-done.4, f32[27,32768]{1,0:T(8,128)S(1)} %fusion.1, f32[32768]{0:T(1024)S(1)} %negate_bitcast_fusion, f32[27]{0:T(128)S(1)} %copy-done.10), kind=kOutput, calls=%fused_computation.1 | convolution fusion | flops 288423936 | bytes 7211984 | tf_op jit(solution)/shard_map/dot_general | solution.py:101
  110.3 0.7 copy.27
  111.1 0.4 slice.431
  111.5 1.8 copy-done
  113.3 3.6 %collective-permute-start = (f32[27,1,32,128]{3,2,1,0:T(8,128)S(1)}, f32[27,1,32,128]{3,2,1,0:T(8,128)S(1)}, u32[]{:S(2)}, u32[]{:S(2)}) collective-permute-start(f32[27,1,32,128]{3,2,1,0:T(8,128)S(1)} %slice.391), channel_id=1, source_target_pairs={{0,4},{4,8},{8,12},{12,16},{16,20},{20,24},{24,28},{28,32},{32,36}... | collective-permute-start | bytes 1327112 | tf_op jit(solution)/shard_map/ppermute | solution.py:17
  116.9 0.7 dynamic_slice.3
  118.3 129.6 %all-gather.2.cloned.1.call-done = f32[27,64,32,128]{3,2,0,1:T(8,128)} async-done(((f32[27,2,32,128]{3,2,0,1:T(8,128)}), f32[27,64,32,128]{3,2,0,1:T(8,128)}) %all-gather.2.cloned.1.call-update) | async-done | bytes 28311568 | tf_op jit(solution)/shard_map/all_gather | solution.py:148
  247.9 31.6 %fusion.26 = f32[27,2,32,128]{3,1,2,0:T(2,128)S(1)} fusion(f32[27,64,32,128]{3,2,0,1:T(8,128)} %all-gather.2.cloned.1.call-done, s32[2]{0:T(128)S(1)} %iota_add_fusion), kind=kOutput, calls=%fused_computation.29 | convolution fusion | flops 169869440 | bytes 29196296 | tf_op jit(solution)/shard_map/pr,kryz->kpyz/dot_general | solution.py:151
  279.5 0.1 copy.24
  279.6 0.1 pad.214
  279.7 0.6 copy.28
  280.4 0.7 fusion.81
  281.1 1.0 fusion.82
  282.1 0.2 copy.29
  282.4 0.3 fusion.29
  282.7 2.7 collective-permute-start.1
  285.4 0.4 slice.393
  285.8 13.2 %collective-permute-done.1 = f32[27,1,32,128]{3,2,1,0:T(8,128)S(1)} collective-permute-done((f32[27,1,32,128]{3,2,1,0:T(8,128)S(1)}, f32[27,1,32,128]{3,2,1,0:T(8,128)S(1)}, u32[]{:S(2)}, u32[]{:S(2)}) %collective-permute-start.1) | collective-permute-done | bytes 442400 | tf_op jit(solution)/shard_map/ppermute | solution.py:19
  299.1 0.2 pad_maximum_fusion
  299.3 2.2 collective-permute-start.3
  301.5 2.0 collective-permute-done.3
  303.5 3.1 collective-permute-done.2
  306.8 0.1 slice.395
  307.0 0.1 slice.400
  307.1 0.1 slice.396
  307.2 0.1 fusion.40
  307.5 0.1 fusion.41
  307.6 0.1 fusion.42
  307.8 0.1 slice.404
  307.9 0.1 fusion.43
  308.1 0.1 fusion.44
  308.3 0.1 slice.411
  308.4 0.1 fusion.45
  308.5 0.1 fusion.46
  308.8 0.1 slice.412
  308.9 0.1 fusion.47
  309.0 0.1 fusion.48
  309.5 0.1 fusion.49
  309.6 0.1 fusion.50
  310.0 0.1 fusion.51
  310.1 0.1 fusion.52
  310.4 0.1 fusion.53
  310.5 0.1 fusion.54
  310.7 0.1 fusion.55
  310.8 0.1 fusion.56
  310.9 0.1 fusion.57
  311.0 1.8 copy-done.8
  (68 shorter events, 2.0 us)
Async XLA Ops:
  7.2 240.7 %all-gather.2.cloned.1.call-start = ((), (), s32[]{:S(2)}) async-start(), calls=%async_computation | async-start | bytes 29196288 | tf_op jit(solution)/shard_map/all_gather | solution.py:148
  11.9 4.4 %copy-start.7 = (s32[512]{0:T(512)S(1)}, s32[512]{0:T(512)}, u32[]{:S(2)}) copy-start(s32[512]{0:T(512)} %param.20) | copy-start | bytes 6148
  11.9 4.4 %copy-start.9 = (s32[512]{0:T(512)S(1)}, s32[512]{0:T(512)}, u32[]{:S(2)}) copy-start(s32[512]{0:T(512)} %param.19) | copy-start | bytes 6148
  11.9 4.5 %copy-start.5 = (f32[27,27]{1,0:T(8,128)S(1)}, f32[27,27]{1,0:T(8,128)}, u32[]{:S(2)}) copy-start(f32[27,27]{1,0:T(8,128)} %constant.89.clone) | copy-start | bytes 8752
  21.7 2.0 copy-start.2
  23.7 74.2 %copy-start.12 = (f32[32]{0:T(128)S(1)}, f32[32]{0:T(128)}, u32[]{:S(2)}) copy-start(f32[32]{0:T(128)} %param.18) | copy-start | bytes 388
  23.7 74.7 %copy-start.13 = (f32[27]{0:T(128)S(1)}, f32[27]{0:T(128)}, u32[]{:S(2)}) copy-start(f32[27]{0:T(128)} %param.17) | copy-start | bytes 328
  23.7 74.8 %copy-start.15 = (f32[27]{0:T(128)S(1)}, f32[27]{0:T(128)}, u32[]{:S(2)}) copy-start(f32[27]{0:T(128)} %constant.88.clone) | copy-start | bytes 328
  23.7 74.8 %copy-start.16 = (f32[27]{0:T(128)S(1)}, f32[27]{0:T(128)}, u32[]{:S(2)}) copy-start(f32[27]{0:T(128)} %constant.87.clone) | copy-start | bytes 328
  23.7 74.8 %copy-start.17 = (f32[27]{0:T(128)S(1)}, f32[27]{0:T(128)}, u32[]{:S(2)}) copy-start(f32[27]{0:T(128)} %constant.86.clone) | copy-start | bytes 328
  98.0 8.1 %copy-start.11 = (f32[32]{0:T(128)}, f32[32]{0:T(128)S(1)}, u32[]{:S(2)}) copy-start(f32[32]{0:T(128)S(1)} %multiply_divide_fusion) | copy-start | bytes 388
  98.5 7.7 %copy-start.4 = (f32[27,27]{1,0:T(8,128)S(1)}, f32[27,27]{1,0:T(8,128)}, u32[]{:S(2)}) copy-start(f32[27,27]{1,0:T(8,128)} %constant.90.clone) | copy-start | bytes 8752
  98.5 7.6 %copy-start.10 = (f32[27]{0:T(128)S(1)}, f32[27]{0:T(128)}, u32[]{:S(2)}) copy-start(f32[27]{0:T(128)} %constant.95) | copy-start | bytes 328
  111.1 5.8 %copy-start.14 = (s32[32]{0:T(128)S(1)}, s32[32]{0:T(128)}, u32[]{:S(2)}) copy-start(s32[32]{0:T(128)} %param.16) | copy-start | bytes 388
  111.5 1.8 copy-start
  113.3 172.5 %collective-permute-start = (f32[27,1,32,128]{3,2,1,0:T(8,128)S(1)}, f32[27,1,32,128]{3,2,1,0:T(8,128)S(1)}, u32[]{:S(2)}, u32[]{:S(2)}) collective-permute-start(f32[27,1,32,128]{3,2,1,0:T(8,128)S(1)} %slice.391), channel_id=1, source_target_pairs={{0,4},{4,8},{8,12},{12,16},{16,20},{20,24},{24,28},{28,32},{32,36}... | collective-permute-start | bytes 1327112 | tf_op jit(solution)/shard_map/ppermute | solution.py:17
  279.5 0.9 copy-start.6
  279.5 1.6 copy-start.3
  280.3 2.0 copy-start.1
  282.7 16.4 %collective-permute-start.1 = (f32[27,1,32,128]{3,2,1,0:T(8,128)S(1)}, f32[27,1,32,128]{3,2,1,0:T(8,128)S(1)}, u32[]{:S(2)}, u32[]{:S(2)}) collective-permute-start(f32[27,1,32,128]{3,2,1,0:T(8,128)S(1)} %slice.394), channel_id=1, source_target_pairs={{4,0},{8,4},{12,8},{16,12},{20,16},{24,20},{28,24},{32,28},{36,32}... | collective-permute-start | bytes 1327112 | tf_op jit(solution)/shard_map/ppermute | solution.py:19
  299.3 4.2 %collective-permute-start.3 = (f32[27,10,1,128]{3,2,1,0:T(1,128)S(1)}, f32[27,10,1,128]{3,2,1,0:T(1,128)S(1)}, u32[]{:S(2)}, u32[]{:S(2)}) collective-permute-start(f32[27,10,1,128]{3,2,1,0:T(1,128)S(1)} %get-tuple-element.27), channel_id=1, source_target_pairs={{0,1},{1,2},{2,3},{3,0},{4,5},{5,6},{6,7},{7,4},{8,9},{9,10},{10,1... | collective-permute-start | bytes 414728 | tf_op jit(solution)/shard_map/ppermute | solution.py:17
  301.5 5.1 %collective-permute-start.2 = (f32[27,10,1,128]{3,2,1,0:T(1,128)S(1)}, f32[27,10,1,128]{3,2,1,0:T(1,128)S(1)}, u32[]{:S(2)}, u32[]{:S(2)}) collective-permute-start(f32[27,10,1,128]{3,2,1,0:T(1,128)S(1)} %get-tuple-element.28), channel_id=1, source_target_pairs={{1,0},{2,1},{3,2},{0,3},{5,4},{6,5},{7,6},{4,7},{9,8},{10,9},{11,1... | collective-permute-start | bytes 414728 | tf_op jit(solution)/shard_map/ppermute | solution.py:19
  311.0 1.8 copy-start.8
Sparse Core Ops, SparseCore 0:
  11.0 236.7 all-gather.1
where the time goes:
time: 320 us
  waiting for transfers between devices  148 us (46%)
  blocking collectives  70.7 us (22%)
  matrix products  51.3 us (16%)
  local copies, waits for them, and re-layouts  20.7 us (6%)
  between operations  15.4 us (5%)
  starting transfers between devices  8.56 us (3%)
  other arithmetic  4.99 us (2%)
    all_gather x1, waiting for transfers between devices, body(): piece = lax.all_gather(precursor, 'gx', axis=1, tiled=True)  130 us
    psum x1, blocking collectives, body(): totals = lax.psum(partial_totals, ('gx', 'gy'))  70.7 us
    dot_general x1, matrix products, body(): jnp.einsum('pr,kryz->kpyz', chosen, piece, precision=FULL_PRECISION)  31.6 us
    unnamed x45, local copies, waits for them, and re-layouts  16.8 us
    ppermute x2, waiting for transfers between devices, extended(): lax.ppermute(head, axis, [((i + 1) % count, i) for i in range(count)])  16.3 us
    dot_general x1, matrix products, relax_cells(): balance_moments = jnp.dot(moment_map, balance, precision=FULL_PRECISION)  7.5 us
  transfers between devices with their start and end apart: 5, of which 4 were waited for; matrix products, arithmetic and copies ran while one was open for 20% of the time, Pallas kernels for 0%

commit v1 on v0

--- a/solution.py
+++ b/solution.py
@@ -145,7 +145,9 @@
     post = relax_cells(tables, moments, rates, force).reshape(comps, width_x, width_y, depth)
     source_tile = pairing[tile_x]
     wanted = source_tile * fringe_width + jnp.arange(fringe_width, dtype=jnp.int32)
-    piece = lax.all_gather(precursor, "gx", axis=1, tiled=True)
+    piece = jnp.concatenate(
+        lax.all_to_all(jnp.stack([precursor] * lax.axis_size("gx")), "gx", 0, 0), axis=1
+    )
     have = jnp.arange(piece.shape[1], dtype=jnp.int32)
     chosen = (wanted[:, None] == have[None, :]).astype(jnp.float32)
     chosen_pops = jnp.einsum("pr,kryz->kpyz", chosen, piece, precision=FULL_PRECISION)

time: 320 us -> 649 us (2.03)
  blocking collectives: 70.7 us -> 517 us
  waiting for transfers between devices: 148 us -> 20.1 us
  local copies, waits for them, and re-layouts: 20.7 us -> 54 us
  matrix products: 51.3 us -> 32.9 us
  between operations: 15.4 us -> 2.03 us
  starting transfers between devices: 8.56 us -> 15.9 us
    psum x1, blocking collectives: 70.7 us -> 517 us  [body(): totals = lax.psum(partial_totals, ('gx', 'gy'))]
    all_gather x1 -> x0, waiting for transfers between devices: 130 us -> none  [body(): piece = lax.all_gather(precursor, 'gx', axis=1, tiled=True)]
    reshape x0 -> x1, local copies, waits for them, and re-layouts: none -> 19.5 us  [body(): jnp.concatenate(lax.all_to_all(jnp.stack([precursor] * lax.axis_size('gx'...]
    dot_general x1, matrix products: 31.6 us -> 13.7 us  [body(): jnp.einsum('pr,kryz->kpyz', chosen, piece, precision=FULL_PRECISION)]
    another operation x0 -> x1, local copies, waits for them, and re-layouts: none -> 14.1 us  [body(): jnp.stack([precursor] * lax.axis_size('gx'))]
    all_to_all x0 -> x1, starting transfers between devices: none -> 8.91 us  [body(): lax.all_to_all(jnp.stack([precursor] * lax.axis_size('gx')), 'gx', 0, 0)]
  transfers between devices with their start and end apart: 5 -> 5, of which waited for: 4 -> 2; matrix products, arithmetic and copies ran while one was open for 20% -> 10% of each run, Pallas kernels for 0% -> 0%
where the time goes in v1:
time: 649 us; the launch traced here: 647 us
  blocking collectives  517 us (80%)
  local copies, waits for them, and re-layouts  54 us (8%)
  matrix products  32.9 us (5%)
  waiting for transfers between devices  20.1 us (3%)
  starting transfers between devices  15.9 us (2%)
    psum x1, blocking collectives, body(): totals = lax.psum(partial_totals, ('gx', 'gy'))  517 us
    ppermute x2, waiting for transfers between devices, extended(): lax.ppermute(head, axis, [((i + 1) % count, i) for i in range(count)])  20 us
    reshape x1, local copies, waits for them, and re-layouts, body(): jnp.concatenate(lax.all_to_all(jnp.stack([precursor] * lax.axis_size('gx'...  19.5 us
    unnamed x45, local copies, waits for them, and re-layouts  16.5 us
    another operation x1, local copies, waits for them, and re-layouts, body(): jnp.stack([precursor] * lax.axis_size('gx'))  14.1 us
    dot_general x1, matrix products, body(): jnp.einsum('pr,kryz->kpyz', chosen, piece, precision=FULL_PRECISION)  13.7 us
  transfers between devices with their start and end apart: 5, of which 2 were waited for; matrix products, arithmetic and copies ran while one was open for 10% of the time, Pallas kernels for 0%

profile of v1, /device:TPU:121, one launch (start us, length us, event | category | flops | bytes accessed | tf_op | source)
XLA Modules:
  0.0 647.2 jit_solution(5856367693554360814)
XLA Ops:
  0.6 1.9 copy.22
  2.5 14.1 %stack.40 = f32[32,27,2,32,128]{4,2,3,1,0:T(2,128)} broadcast(f32[27,2,32,128]{3,1,2,0:T(2,128)S(1)} %copy.22), dimensions={1,2,3,4} | broadcast | bytes 29196288 | tf_op jit(solution)/shard_map/stack | solution.py:149
  16.6 8.9 %all-to-all-start = ((f32[32,27,2,32,128]{4,2,3,1,0:T(2,128)}), f32[32,27,2,32,128]{4,2,3,1,0:T(2,128)}, u32[]{:S(2)}, u32[]{:S(2)}) async-start(f32[32,27,2,32,128]{4,2,3,1,0:T(2,128)} %stack.40), calls=%async_computation | async-start | bytes 56623104 | tf_op jit(solution)/shard_map/all_to_all | solution.py:149
  25.6 2.4 pad.213
  28.0 4.4 copy.26
  32.5 5.4 fusion.75
  37.9 2.0 copy-done.2
  39.9 0.5 add_multiply_fusion
  40.5 1.0 gather_fusion
  41.5 0.3 fusion.61
  41.8 0.2 convolution_bitcast_fusion.2
  42.0 517.3 %psum.7 = f32[32]{0:T(128)S(1)} all-reduce(f32[32]{0:T(128)S(1)} %convolution_bitcast_fusion.2), channel_id=1, replica_groups=mesh['gx'=32,'gy'=4] {'gx','gy'}, use_global_device_ids=true, to_apply=%region_0.1 | all-reduce | flops 32 | bytes 256 | tf_op jit(solution)/shard_map/psum | solution.py:134
  559.3 0.6 fusion.68
  559.9 0.1 convert_reduce_fusion
  560.0 0.7 multiply_divide_fusion
  560.7 0.1 convolution_bitcast_fusion.1
  560.9 0.3 fusion.26
  561.3 7.4 %fusion.1 = f32[27,32768]{1,0:T(8,128)S(1)} fusion(f32[27,32768]{1,0:T(8,128)} %copy-done.2, f32[27,27]{1,0:T(8,128)S(1)} %copy-done.5, f32[32768]{0:T(1024)S(1)} %bitcast.254, f32[32768]{0:T(1024)S(1)} %bitcast.256, f32[27]{0:T(128)S(1)} %copy-done.17, f32[32768]{0:T(1024)S(1)} %bitcast.255, f32[27]{0:T(128)S(1)} %copy-done.16, f32[32768]{0:T(1024)S(1)} %bitcast.221, ...), kind=kOutput, calls=%fused_computation.4 | convolution fusion | flops 299925504 | bytes 7736596 | tf_op jit(solution)/shard_map/dot_general | solution.py:98
  568.7 0.1 negate_bitcast_fusion
  568.9 3.8 convolution_add_fusion
  572.7 0.7 copy.27
  573.4 0.4 slice.431
  573.8 1.8 copy-done
  575.6 4.5 collective-permute-start
  580.2 0.6 dynamic_slice.3
  581.4 19.5 %copy.23 = f32[27,32,2,32,128]{4,2,1,3,0:T(2,128)} copy(f32[27,32,2,32,128]{4,2,3,0,1:T(2,128)} %bitcast.18) | data formatting | bytes 56623104 | tf_op jit(solution)/shard_map/reshape | solution.py:148
  600.9 13.7 %convolution_bitcast_fusion = f32[27,2,32,128]{3,1,2,0:T(2,128)S(1)} fusion(f32[27,64,32,128]{3,1,2,0:T(8,128)} %bitcast.219, s32[2]{0:T(128)S(1)} %iota_add_fusion), kind=kOutput, calls=%fused_computation.27 | convolution fusion | flops 169869440 | bytes 29196296 | tf_op jit(solution)/shard_map/pr,kryz->kpyz/dot_general | solution.py:153
  614.6 0.1 copy.24
  614.7 0.1 pad.214
  614.8 0.6 copy.28
  615.5 0.7 fusion.76
  616.2 1.0 fusion.77
  617.2 0.2 copy.29
  617.5 0.3 fusion.24
  617.9 0.4 slice.393
  618.3 16.1 %collective-permute-done.1 = f32[27,1,32,128]{3,2,1,0:T(8,128)S(1)} collective-permute-done((f32[27,1,32,128]{3,2,1,0:T(8,128)S(1)}, f32[27,1,32,128]{3,2,1,0:T(8,128)S(1)}, u32[]{:S(2)}, u32[]{:S(2)}) %collective-permute-start.1) | collective-permute-done | bytes 442400 | tf_op jit(solution)/shard_map/ppermute | solution.py:19
  634.4 0.2 pad_maximum_fusion
  634.6 1.8 collective-permute-start.2
  636.4 0.6 collective-permute-start.3
  637.0 3.9 collective-permute-done.2
  641.2 0.1 slice.399
  641.3 0.1 slice.400
  641.4 0.1 fusion.35
  641.6 0.1 fusion.36
  641.7 0.1 fusion.37
  642.0 0.1 slice.403
  642.1 0.1 slice.408
  642.3 0.1 fusion.38
  642.4 0.1 fusion.39
  642.6 0.1 fusion.40
  642.7 0.1 fusion.41
  643.1 0.1 fusion.42
  643.2 0.1 fusion.43
  643.5 0.1 slice.420
  643.8 0.1 fusion.44
  643.9 0.1 fusion.45
  644.0 0.1 fusion.46
  644.2 0.1 fusion.47
  644.8 0.1 fusion.48
  644.9 0.1 fusion.49
  645.0 0.1 fusion.50
  645.1 0.1 fusion.51
  645.3 0.1 fusion.52
  645.4 1.8 copy-done.8
  (69 shorter events, 2.1 us)
Async XLA Ops:
  16.6 564.8 %all-to-all-start = ((f32[32,27,2,32,128]{4,2,3,1,0:T(2,128)}), f32[32,27,2,32,128]{4,2,3,1,0:T(2,128)}, u32[]{:S(2)}, u32[]{:S(2)}) async-start(f32[32,27,2,32,128]{4,2,3,1,0:T(2,128)} %stack.40), calls=%async_computation | async-start | bytes 56623104 | tf_op jit(solution)/shard_map/all_to_all | solution.py:149
  28.0 4.5 copy-start.7
  28.0 4.5 copy-start.9
  28.0 4.5 copy-start.5
  37.9 2.0 copy-start.2
  39.9 520.8 %copy-start.12 = (f32[32]{0:T(128)S(1)}, f32[32]{0:T(128)}, u32[]{:S(2)}) copy-start(f32[32]{0:T(128)} %param.18) | copy-start | bytes 388
  39.9 521.3 %copy-start.13 = (f32[27]{0:T(128)S(1)}, f32[27]{0:T(128)}, u32[]{:S(2)}) copy-start(f32[27]{0:T(128)} %param.17) | copy-start | bytes 328
  39.9 521.3 %copy-start.15 = (f32[27]{0:T(128)S(1)}, f32[27]{0:T(128)}, u32[]{:S(2)}) copy-start(f32[27]{0:T(128)} %constant.86.clone) | copy-start | bytes 328
  39.9 521.3 %copy-start.16 = (f32[27]{0:T(128)S(1)}, f32[27]{0:T(128)}, u32[]{:S(2)}) copy-start(f32[27]{0:T(128)} %constant.87.clone) | copy-start | bytes 328
  39.9 521.3 %copy-start.17 = (f32[27]{0:T(128)S(1)}, f32[27]{0:T(128)}, u32[]{:S(2)}) copy-start(f32[27]{0:T(128)} %constant.88.clone) | copy-start | bytes 328
  560.7 8.0 %copy-start.11 = (f32[32]{0:T(128)}, f32[32]{0:T(128)S(1)}, u32[]{:S(2)}) copy-start(f32[32]{0:T(128)S(1)} %multiply_divide_fusion) | copy-start | bytes 388
  561.3 7.6 %copy-start.4 = (f32[27,27]{1,0:T(8,128)S(1)}, f32[27,27]{1,0:T(8,128)}, u32[]{:S(2)}) copy-start(f32[27,27]{1,0:T(8,128)} %constant.90.clone) | copy-start | bytes 8752
  561.3 7.6 %copy-start.10 = (f32[27]{0:T(128)S(1)}, f32[27]{0:T(128)}, u32[]{:S(2)}) copy-start(f32[27]{0:T(128)} %constant.95) | copy-start | bytes 328
  573.4 6.7 %copy-start.14 = (s32[32]{0:T(128)S(1)}, s32[32]{0:T(128)}, u32[]{:S(2)}) copy-start(s32[32]{0:T(128)} %param.16) | copy-start | bytes 388
  573.8 1.8 copy-start
  575.6 42.6 %collective-permute-start = (f32[27,1,32,128]{3,2,1,0:T(8,128)S(1)}, f32[27,1,32,128]{3,2,1,0:T(8,128)S(1)}, u32[]{:S(2)}, u32[]{:S(2)}) collective-permute-start(f32[27,1,32,128]{3,2,1,0:T(8,128)S(1)} %slice.391), channel_id=1, source_target_pairs={{0,4},{4,8},{8,12},{12,16},{16,20},{20,24},{24,28},{28,32},{32,36}... | collective-permute-start | bytes 1327112 | tf_op jit(solution)/shard_map/ppermute | solution.py:17
  614.6 0.9 copy-start.6
  614.6 1.6 copy-start.3
  615.5 2.0 copy-start.1
  617.8 16.6 %collective-permute-start.1 = (f32[27,1,32,128]{3,2,1,0:T(8,128)S(1)}, f32[27,1,32,128]{3,2,1,0:T(8,128)S(1)}, u32[]{:S(2)}, u32[]{:S(2)}) collective-permute-start(f32[27,1,32,128]{3,2,1,0:T(8,128)S(1)} %slice.394), channel_id=1, source_target_pairs={{4,0},{8,4},{12,8},{16,12},{20,16},{24,20},{28,24},{32,28},{36,32}... | collective-permute-start | bytes 1327112 | tf_op jit(solution)/shard_map/ppermute | solution.py:19
  634.6 6.3 collective-permute-start.2
  636.4 4.5 collective-permute-start.3
  645.4 1.8 copy-start.8
